TPU v7x, 32 devices: a whole 2x2x4 slice. The times are simulated.
32 devices in a mesh: dp: 4 (over x, core), expert: 8 (over z, y).
Axes of the slice: x: 2, y: 2, z: 4, core: 2. Of those that a mesh axis runs over, the one named last changes fastest.
Arguments:
- tokens: bfloat16 [2048, 2048], P(('dp', 'expert')), may hold values from -6 to 6
- gate_values: float32 [2048, 4], P(('dp', 'expert')), may hold values from 0.1 to 1
- chosen: int32 [2048, 4], P(('dp', 'expert')), may hold values from 0 to 63, all different within a row; in each aligned block of 64 rows (0 to 63, 64 to 127, ...) at most 8 rows name the same one
- slot_table: int32 [64], replicated, may hold values from 0 to 63, each once
- w_gate: bfloat16 [64, 768, 2048], P('expert', 'dp'), may hold values from -0.125 to 0.125
- w_up: bfloat16 [64, 768, 2048], P('expert', 'dp'), may hold values from -0.125 to 0.125
- w_down: bfloat16 [64, 768, 2048], P('expert', 'dp'), may hold values from -0.21875 to 0.21875
- cotangent: bfloat16 [2048, 2048], P(('dp', 'expert')), may hold values from -0.59765625 to 0.59765625
Outputs:
- mixed: bfloat16 [2048, 2048], P(('dp', 'expert'))
- token_grads: bfloat16 [2048, 2048], P(('dp', 'expert'))
- gate_grads: float32 [2048, 4], P(('dp', 'expert'))
- gate_weight_grad: bfloat16 [64, 768, 2048], P('expert', 'dp')
- up_weight_grad: bfloat16 [64, 768, 2048], P('expert', 'dp')
- down_weight_grad: bfloat16 [64, 768, 2048], P('expert', 'dp')
Inputs may be any that keep to these rules, and one draw needn't show every extreme that they name: `chosen`: each row names 4 distinct experts. Within the rows of one device (aligned blocks of 64 tokens) no expert is named by more than 8 rows, and in every draw some expert is named by exactly 8 rows of some block. `slot_table`: A permutation of the storage indices.
All inputs are finite; a program needn't handle non-finite values.
Results may differ from a plain program's by a relative error of at most 0.009.
Values may be sent and summed in bfloat16 or wider, within the bound.
A program may use at most 384 MiB of HBM per device.

v0:
```python
import jax
import jax.numpy as jnp
from jax import lax
from jax.sharding import PartitionSpec as P

CAP = 8
PAD = 128
F32 = jnp.float32
BF16 = jnp.bfloat16
AXES = ("dp", "expert")


def split3(v):
    a = lax.reduce_precision(v, 8, 7)
    r = v - a
    b = lax.reduce_precision(r, 8, 7)
    return (a.astype(BF16), b.astype(BF16), (r - b).astype(BF16))


def per_device(tokens, gate_values, chosen, slot_table, w_gate, w_up, w_down, cotangent):
    tok, width = tokens.shape
    topk = chosen.shape[1]
    experts = slot_table.shape[0]
    groups = lax.axis_size("expert")
    n_dev = groups * lax.axis_size("dp")
    per_dev = w_gate.shape[0]
    blocks = max(1, min(n_dev, 256 // tok))
    chunks = n_dev // blocks
    labels = jnp.arange(experts, dtype=jnp.int32)
    slot = jnp.sum(jnp.where(chosen[:, :, None] == labels, slot_table, 0), axis=2)
    named = jnp.sum((slot[:, :, None] == labels).astype(F32), axis=1)
    lower = (jnp.arange(tok)[:, None] > jnp.arange(tok)[None, :]).astype(F32)
    before = jnp.dot(lower, named, preferred_element_type=F32)
    pos = jnp.sum(jnp.where(slot[:, :, None] == labels, before[:, None, :], 0.0), axis=2)
    g1, g2, g3 = split3(gate_values)
    extra = jnp.concatenate([slot.astype(BF16), pos.astype(BF16), g1, g2, g3], axis=1)
    extra = jnp.pad(extra, ((0, 0), (0, PAD - extra.shape[1])))
    packed = jnp.concatenate([tokens, cotangent, extra], axis=1)
    allp = lax.all_gather(packed, AXES, axis=0, tiled=True)
    allp = allp.reshape(chunks, blocks * tok, 2 * width + PAD)
    x_all = allp[:, :, :width]
    c_all = allp[:, :, width : 2 * width]
    ex = allp[:, :, 2 * width : 2 * width + 5 * topk].astype(F32)
    ex = ex.reshape(chunks, blocks * tok, 5, topk)
    slot_all = ex[:, :, 0].astype(jnp.int32) - lax.axis_index("expert") * per_dev
    pos_all = ex[:, :, 1].astype(jnp.int32)
    gate_all = ex[:, :, 2] + ex[:, :, 3] + ex[:, :, 4]
    blk = (jnp.arange(blocks * tok, dtype=jnp.int32) // tok)[None, :, None]
    rows = blocks * CAP
    here = (slot_all >= 0) & (slot_all < per_dev)
    row_id = jnp.where(here, slot_all * rows + blk * CAP + pos_all, -1)
    rid = jnp.arange(per_dev * rows, dtype=jnp.int32)[None, :, None, None]
    match = row_id[:, None, :, :] == rid
    sel = jnp.sum(match.astype(F32), axis=3).astype(BF16)
    gate_row = jnp.sum(jnp.where(match, gate_all[:, None], 0.0), axis=(2, 3))

    def to_expert(v):
        v = v.reshape((chunks, per_dev, rows) + v.shape[2:])
        v = jnp.swapaxes(v, 0, 1)
        return v.reshape((per_dev, chunks * rows) + v.shape[3:])

    def to_chunk(v):
        v = v.reshape((per_dev, chunks, rows) + v.shape[2:])
        v = jnp.swapaxes(v, 0, 1)
        return v.reshape((chunks, per_dev * rows) + v.shape[3:])

    x_rows = to_expert(
        jnp.einsum("crt,ctd->crd", sel, x_all, preferred_element_type=F32).astype(BF16)
    )
    c_rows = to_expert(
        jnp.einsum("crt,ctd->crd", sel, c_all, preferred_element_type=F32).astype(BF16)
    )
    gate_e = to_expert(gate_row)[:, :, None]
    pre_gate = jnp.einsum("erd,efd->erf", x_rows, w_gate, preferred_element_type=F32)
    pre_up = jnp.einsum("erd,efd->erf", x_rows, w_up, preferred_element_type=F32)
    dh = jnp.einsum("erd,efd->erf", c_rows, w_down, preferred_element_type=F32)
    s = jax.nn.sigmoid(pre_gate)
    act = pre_gate * s
    hid = act * pre_up
    gg_row = jnp.sum(hid * dh, axis=2)
    hid = (hid * gate_e).astype(BF16)
    dh = dh * gate_e
    grad_gate = (dh * pre_up * s * (1.0 + pre_gate * (1.0 - s))).astype(BF16)
    grad_up = (dh * act).astype(BF16)
    out_rows = jnp.einsum("erf,efd->erd", hid, w_down, preferred_element_type=F32).astype(BF16)
    back_rows = (
        jnp.einsum("erf,efd->erd", grad_gate, w_gate, preferred_element_type=F32)
        + jnp.einsum("erf,efd->erd", grad_up, w_up, preferred_element_type=F32)
    ).astype(BF16)
    dw_gate = jnp.einsum("erf,erd->efd", grad_gate, x_rows, preferred_element_type=F32).astype(BF16)
    dw_up = jnp.einsum("erf,erd->efd", grad_up, x_rows, preferred_element_type=F32).astype(BF16)
    dw_down = jnp.einsum("erf,erd->efd", hid, c_rows, preferred_element_type=F32).astype(BF16)
    part_m = jnp.einsum("crt,crd->ctd", sel, to_chunk(out_rows), preferred_element_type=F32)
    part_b = jnp.einsum("crt,crd->ctd", sel, to_chunk(back_rows), preferred_element_type=F32)
    gg_c = to_chunk(gg_row)
    part_g = jnp.sum(jnp.where(match, gg_c[:, :, None, None], 0.0), axis=1)
    part_g = jnp.pad(part_g, ((0, 0), (0, 0), (0, PAD - topk)))
    part = jnp.concatenate([part_m.astype(BF16), part_b.astype(BF16), part_g.astype(BF16)], axis=2)
    part = part.reshape(n_dev * tok, 2 * width + PAD)
    red = lax.psum_scatter(part, AXES, scatter_dimension=0, tiled=True)
    return (
        red[:, :width],
        red[:, width : 2 * width],
        red[:, 2 * width : 2 * width + topk].astype(F32),
        dw_gate,
        dw_up,
        dw_down,
    )


def solution(mesh):
    tok = P(AXES, None)
    w = P("expert", "dp", None)
    return jax.shard_map(
        per_device,
        mesh=mesh,
        in_specs=(tok, tok, tok, P(), w, w, w, tok),
        out_specs=(tok, tok, tok, w, w, w),
        check_vma=False,
    )
```

profile of v0, /device:TPU:0, one launch (start us, length us, event | category | flops | bytes accessed | tf_op | source)
XLA Modules:
  0.0 495.5 jit_solution(17342932502256121510)
XLA Ops:
  9.5 1.9 fusion.14
  11.4 119.7 %all-gather.2.cloned.1.call-done = bf16[2048,4224]{1,0:T(8,128)(2,1)} async-done(((bf16[64,4224]{1,0:T(8,128)(2,1)}), bf16[2048,4224]{1,0:T(8,128)(2,1)}) %all-gather.2.cloned.1.call-update) | async-done | bytes 17301520 | tf_op jit(solution)/shard_map/all_gather | solution.py:39
  133.6 9.0 %fusion.6 = bf16[8,256,2048]{2,1,0:T(8,128)(2,1)} fusion(bf16[8,256,256]{2,1,0:T(8,128)(2,1)S(1)} %convert_reduce_fusion, bf16[8,256,4224]{2,1,0:T(8,128)(2,1)} %bitcast.75), kind=kOutput, calls=%fused_computation.13 | convolution fusion | flops 2151677952 | bytes 17825792 | tf_op jit(solution)/shard_map/crt,ctd->crd/dot_general | solution.py:68
  142.6 9.0 %fusion.9 = bf16[8,256,2048]{2,1,0:T(8,128)(2,1)} fusion(bf16[8,256,256]{2,1,0:T(8,128)(2,1)S(1)} %convert_reduce_fusion, bf16[8,256,4224]{2,1,0:T(8,128)(2,1)} %bitcast.76), kind=kOutput, calls=%fused_computation.14 | convolution fusion | flops 2151677952 | bytes 17825792 | tf_op jit(solution)/shard_map/crt,ctd->crd/dot_general | solution.py:71
  151.7 8.3 %copy.96 = bf16[8,8,32,2048]{3,2,1,0:T(8,128)(2,1)} copy(bf16[8,8,32,2048]{3,2,0,1:T(8,128)(2,1)} %bitcast.69) | data formatting | bytes 16777216 | tf_op jit(solution)/shard_map/transpose | solution.py:59
  160.0 8.2 %fusion.24 = f32[8,256,192]{1,2,0:T(8,128)S(1)} fusion(bf16[8,256,2048]{2,1,0:T(8,128)(2,1)} %bitcast.62, bf16[8,192,2048]{2,1,0:T(8,128)(2,1)} %param.12), kind=kOutput, calls=%fused_computation.58 | convolution fusion | flops 1610612736 | bytes 16252928 | tf_op jit(solution)/shard_map/erd,efd->erf/dot_general | solution.py:74
  168.2 7.6 %fusion.25 = f32[8,256,192]{1,2,0:T(8,128)} fusion(bf16[8,256,2048]{2,1,0:T(8,128)(2,1)S(1)} %bitcast.65, bf16[8,192,2048]{2,1,0:T(8,128)(2,1)} %param.13), kind=kOutput, calls=%fused_computation.59 | convolution fusion | flops 1610612736 | bytes 16252928 | tf_op jit(solution)/shard_map/erd,efd->erf/dot_general | solution.py:75
  175.8 19.6 %copy.102 = bf16[8,8,32,2048]{3,2,1,0:T(8,128)(2,1)} copy(bf16[8,8,32,2048]{3,2,0,1:T(8,128)(2,1)} %bitcast.68) | data formatting | bytes 16777216 | tf_op jit(solution)/shard_map/transpose | solution.py:59
  195.5 9.6 %multiply_reduce_fusion = (f32[8,256]{1,0:T(8,128)S(1)}, f32[8,256,192]{1,2,0:T(8,128)}) fusion(f32[8,256,192]{1,2,0:T(8,128)S(1)} %copy-done.3, f32[8,256,192]{1,2,0:T(8,128)S(1)} %fusion.24, bf16[8,256,2048]{2,1,0:T(8,128)(2,1)} %bitcast.72, bf16[8,192,2048]{2,1,0:T(8,128)(2,1)} %param.14), kind=kOutput, calls=%fused_computation.20 | convolution fusion | flops 1613363200 | bytes 19406848 | tf_op jit(solution)/shard_map/erd,efd->erf/dot_general | solution.py:76
  205.3 2.6 select_reduce_fusion.1
  208.0 4.2 multiply_convert_fusion.2
  212.2 10.9 %fusion.26 = f32[8,256,2048]{2,1,0:T(8,128)} fusion(bf16[8,256,192]{1,2,0:T(8,128)(2,1)S(1)} %get-tuple-element.45, bf16[8,192,2048]{2,1,0:T(8,128)(2,1)} %param.12), kind=kOutput, calls=%fused_computation.60 | convolution fusion | flops 1610612736 | bytes 23855104 | tf_op jit(solution)/shard_map/erf,efd->erd/dot_general | solution.py:87
  223.1 13.5 %add_convert_fusion = bf16[8,256,2048]{2,1,0:T(8,128)(2,1)} fusion(f32[8,256,2048]{2,1,0:T(8,128)} %fusion.26, bf16[8,256,192]{1,2,0:T(8,128)(2,1)} %get-tuple-element.46, bf16[8,192,2048]{2,1,0:T(8,128)(2,1)} %param.13), kind=kOutput, calls=%fused_computation.3 | convolution fusion | flops 1619001344 | bytes 32243712 | tf_op jit(solution)/shard_map/erf,efd->erd/dot_general | solution.py:88
  236.6 8.4 %copy.103 = bf16[8,8,32,2048]{3,2,1,0:T(8,128)(2,1)} copy(bf16[8,8,32,2048]{3,2,0,1:T(8,128)(2,1)} %bitcast.77) | data formatting | bytes 16777216 | tf_op jit(solution)/shard_map/transpose | solution.py:64
  245.0 9.2 %convolution_convert_fusion.1 = bf16[8,256,2048]{2,1,0:T(8,128)(2,1)} fusion(bf16[8,256,256]{2,1,0:T(8,128)(2,1)S(1)} %convert_reduce_fusion, bf16[8,256,2048]{2,1,0:T(8,128)(2,1)} %bitcast.71), kind=kOutput, calls=%fused_computation.15 | convolution fusion | flops 2151677952 | bytes 17825792 | tf_op jit(solution)/shard_map/crt,crd->ctd/dot_general | solution.py:94
  254.2 5.7 %convolution_convert_fusion = bf16[8,256,2048]{2,1,0:T(8,128)(2,1)} fusion(bf16[8,256,192]{1,2,0:T(8,128)(2,1)S(1)} %get-tuple-element.44, bf16[8,192,2048]{2,1,0:T(8,128)(2,1)S(1)} %bitcast.79), kind=kOutput, calls=%fused_computation.12 | convolution fusion | flops 1614807040 | bytes 15466496 | tf_op jit(solution)/shard_map/erf,efd->erd/dot_general | solution.py:85
  259.9 8.4 %copy.99 = bf16[8,8,32,2048]{3,2,1,0:T(8,128)(2,1)} copy(bf16[8,8,32,2048]{3,2,0,1:T(8,128)(2,1)} %bitcast.67) | data formatting | bytes 16777216 | tf_op jit(solution)/shard_map/transpose | solution.py:64
  268.3 9.0 %convolution_convert_fusion.2 = bf16[8,256,2048]{2,1,0:T(8,128)(2,1)} fusion(bf16[8,256,256]{2,1,0:T(8,128)(2,1)S(1)} %convert_reduce_fusion, bf16[8,256,2048]{2,1,0:T(8,128)(2,1)} %bitcast.70), kind=kOutput, calls=%fused_computation.16 | convolution fusion | flops 2151677952 | bytes 17825792 | tf_op jit(solution)/shard_map/crt,crd->ctd/dot_general | solution.py:93
  277.6 13.9 %fusion.1 = bf16[8,256,4224]{2,1,0:T(8,128)(2,1)} fusion(bf16[8,256,4]{2,1,0:T(8,128)(2,1)S(1)} %copy.123, bf16[8,256,2048]{2,1,0:T(8,128)(2,1)} %convolution_convert_fusion.1, bf16[8,256,2048]{2,1,0:T(8,128)(2,1)} %convolution_convert_fusion.2), kind=kLoop, calls=%fused_computation.2 | loop fusion | flops 69206016 | bytes 34095104 | tf_op jit(solution)/shard_map/concatenate | solution.py:98
  291.5 8.0 %convolution_convert_fusion.3 = bf16[8,192,2048]{2,1,0:T(8,128)(2,1)} fusion(bf16[8,256,192]{1,2,0:T(8,128)(2,1)S(1)} %get-tuple-element.44, bf16[8,256,2048]{2,1,0:T(8,128)(2,1)} %bitcast.73), kind=kOutput, calls=%fused_computation.17 | convolution fusion | flops 1613758464 | bytes 15466496 | tf_op jit(solution)/shard_map/erf,erd->efd/dot_general | solution.py:92
  299.5 8.5 %convolution_convert_fusion.4 = bf16[8,192,2048]{2,1,0:T(8,128)(2,1)} fusion(bf16[8,256,192]{1,2,0:T(8,128)(2,1)S(1)} %copy-done.1, bf16[8,256,2048]{2,1,0:T(8,128)(2,1)} %bitcast.63), kind=kOutput, calls=%fused_computation.18 | convolution fusion | flops 1613758464 | bytes 15466496 | tf_op jit(solution)/shard_map/erf,erd->efd/dot_general | solution.py:91
  308.0 8.5 %convolution_convert_fusion.5 = bf16[8,192,2048]{2,1,0:T(8,128)(2,1)} fusion(bf16[8,256,192]{1,2,0:T(8,128)(2,1)S(1)} %get-tuple-element.45, bf16[8,256,2048]{2,1,0:T(8,128)(2,1)} %bitcast.64), kind=kOutput, calls=%fused_computation.19 | convolution fusion | flops 1613758464 | bytes 15466496 | tf_op jit(solution)/shard_map/erf,erd->efd/dot_general | solution.py:90
  316.5 168.5 %reduce-scatter.4.cloned.1.call-done = bf16[64,4224]{1,0:T(8,128)(2,1)} async-done(((bf16[2048,4224]{1,0:T(8,128)(2,1)}), bf16[64,4224]{1,0:T(8,128)(2,1)}) %reduce-scatter.4.cloned.1.call-update) | async-done | bytes 540688
  486.4 1.9 fusion.23
  (45 shorter events, 7.0 us)
Async XLA Ops:
  7.2 123.9 %all-gather.2.cloned.1.call-start = ((), (), s32[]{:S(2)}) async-start(), calls=%async_computation.1 | async-start | bytes 17842176 | tf_op jit(solution)/shard_map/all_gather | solution.py:39
  11.3 473.7 %reduce-scatter.4.cloned.1.call-start = ((), (), s32[]{:S(2)}) async-start(), calls=%async_computation.2 | async-start | bytes 17842176
  160.0 8.2 %copy-start = (bf16[8,8,32,2048]{3,2,1,0:T(8,128)(2,1)S(1)}, bf16[8,8,32,2048]{3,2,1,0:T(8,128)(2,1)}, u32[]{:S(2)}) copy-start(bf16[8,8,32,2048]{3,2,1,0:T(8,128)(2,1)} %copy.96) | copy-start | bytes 25165828
  168.2 27.3 %copy-start.2 = (f32[8,256,192]{1,2,0:T(8,128)}, f32[8,256,192]{1,2,0:T(8,128)S(1)}, u32[]{:S(2)}) copy-start(f32[8,256,192]{1,2,0:T(8,128)S(1)} %fusion.24) | copy-start | bytes 4718596
  175.8 19.7 %copy-start.3 = (f32[8,256,192]{1,2,0:T(8,128)S(1)}, f32[8,256,192]{1,2,0:T(8,128)}, u32[]{:S(2)}) copy-start(f32[8,256,192]{1,2,0:T(8,128)} %fusion.25) | copy-start | bytes 4718596
  236.6 17.6 %slice-start = ((s8[6291456]{0:T(1024)(128)(4,1)}), s8[2097152]{0:T(1024)(128)(4,1)S(1)}, s32[]{:S(2)}) async-start(s8[6291456]{0:T(1024)(128)(4,1)} %bitcast.78), calls=%async_computation.3 | async-start | bytes 4194304
  245.0 9.2 %slice-start.1 = ((s8[6291456]{0:T(1024)(128)(4,1)}), s8[4194304]{0:T(1024)(128)(4,1)S(1)}, s32[]{:S(2)}) async-start(s8[6291456]{0:T(1024)(128)(4,1)} %bitcast.78), calls=%async_computation.4 | async-start | bytes 8388608
  291.5 8.0 %copy-start.1 = (bf16[8,256,192]{1,2,0:T(8,128)(2,1)S(1)}, bf16[8,256,192]{1,2,0:T(8,128)(2,1)}, u32[]{:S(2)}) copy-start(bf16[8,256,192]{1,2,0:T(8,128)(2,1)} %get-tuple-element.46) | copy-start | bytes 2359300
Sparse Core Ops, SparseCore 0:
  11.5 119.5 all-gather.1
  291.6 193.3 reduce-scatter.3
where the time goes:
time: 505 us; the launch traced here: 496 us
  waiting for transfers between devices  288 us (57%)
  matrix products  117 us (23%)
  local copies, waits for them, and re-layouts  49.7 us (10%)
  other arithmetic  26.3 us (5%)
  between operations  14.5 us (3%)
    unnamed x3, waiting for transfers between devices  169 us
    all_gather x1, waiting for transfers between devices, per_device(): allp = lax.all_gather(packed, AXES, axis=0, tiled=True)  120 us
    transpose x3, local copies, waits for them, and re-layouts, to_expert(): v = jnp.swapaxes(v, 0, 1)  28 us
    transpose x3, local copies, waits for them, and re-layouts, to_chunk(): v = jnp.swapaxes(v, 0, 1)  16.9 us
    concatenate x1, other arithmetic, per_device(): jnp.concatenate([part_m.astype(BF16), part_b.astype(BF16), part_g.astype(...  13.9 us
    dot_general x1, matrix products, per_device(): jnp.einsum('erf,efd->erd', grad_up, w_up, preferred_element_type=F32)  13.5 us
    dot_general x1, matrix products, per_device(): jnp.einsum('erf,efd->erd', grad_gate, w_gate, preferred_element_type=F32)  10.9 us
  transfers between devices with their start and end apart: 2, of which 2 were waited for; matrix products, arithmetic and copies ran while one was open for 5% of the time, Pallas kernels for 0%

commit v1 on v0

--- a/solution.py
+++ b/solution.py
@@ -8,6 +8,18 @@
 F32 = jnp.float32
 BF16 = jnp.bfloat16
 AXES = ("dp", "expert")
+
+
+def gather_by_bits(shard, axis, dim):
+    ways, here, lap = (lax.axis_size(axis), lax.axis_index(axis), shard.shape[dim])
+    line, have = (shard, 1)
+    while have < ways:
+        line = jnp.concatenate(
+            [line, lax.ppermute(line, axis, [(d, (d - have) % ways) for d in range(ways)])],
+            axis=dim,
+        )
+        have = 2 * have
+    return jnp.roll(line, here * lap, axis=dim)
 
 
 def split3(v):
@@ -36,7 +48,7 @@
     extra = jnp.concatenate([slot.astype(BF16), pos.astype(BF16), g1, g2, g3], axis=1)
     extra = jnp.pad(extra, ((0, 0), (0, PAD - extra.shape[1])))
     packed = jnp.concatenate([tokens, cotangent, extra], axis=1)
-    allp = lax.all_gather(packed, AXES, axis=0, tiled=True)
+    allp = gather_by_bits(packed, AXES, 0)
     allp = allp.reshape(chunks, blocks * tok, 2 * width + PAD)
     x_all = allp[:, :, :width]
     c_all = allp[:, :, width : 2 * width]

time: 505 us -> 809 us (1.60)
  waiting for transfers between devices: 288 us -> 540 us
  local copies, waits for them, and re-layouts: 49.7 us -> 83.2 us
  starting transfers between devices: 0.08 us -> 9.08 us
    ppermute x0 -> x5, waiting for transfers between devices: none -> 362 us  [gather_by_bits(): lax.ppermute(line, axis, [(d, (d - have) % ways) for d in range(ways)])]
    all_gather x1 -> x0, waiting for transfers between devices: 120 us -> none  [per_device(): allp = lax.all_gather(packed, AXES, axis=0, tiled=True)]
    unnamed x16 -> x42, local copies, waits for them, and re-layouts: 0.78 us -> 26.9 us
    transpose x3, local copies, waits for them, and re-layouts: 28 us -> 16.6 us  [to_expert(): v = jnp.swapaxes(v, 0, 1)]
    concatenate x0 -> x2, local copies, waits for them, and re-layouts: none -> 11.3 us  [the longest x1 7.38 us: gather_by_bits(): return jnp.roll(line, here * lap, axis=dim)]
    dot_general x1, matrix products: 7.62 us -> 18.9 us  [per_device(): jnp.einsum('erd,efd->erf', x_rows, w_up, preferred_element_type=F32)]
    unnamed x3 -> x2, waiting for transfers between devices: 169 us -> 178 us
    ppermute x0 -> x5, starting transfers between devices: none -> 9.04 us  [gather_by_bits(): lax.ppermute(line, axis, [(d, (d - have) % ways) for d in range(ways)])]
  transfers between devices with their start and end apart: 2 -> 6, of which waited for: 2 -> 6; matrix products, arithmetic and copies ran while one was open for 5% -> 3% of each run, Pallas kernels for 0% -> 0%
where the time goes in v1:
time: 809 us; the launch traced here: 804 us
  waiting for transfers between devices  540 us (67%)
  matrix products  125 us (15%)
  local copies, waits for them, and re-layouts  83.2 us (10%)
  other arithmetic  32.1 us (4%)
  between operations  14.5 us (2%)
  starting transfers between devices  9.08 us (1%)
    ppermute x5, waiting for transfers between devices, gather_by_bits(): lax.ppermute(line, axis, [(d, (d - have) % ways) for d in range(ways)])  362 us
    unnamed x2, waiting for transfers between devices  178 us
    unnamed x42, local copies, waits for them, and re-layouts  26.9 us
    dot_general x1, matrix products, per_device(): jnp.einsum('erd,efd->erf', x_rows, w_up, preferred_element_type=F32)  18.9 us
    transpose x3, local copies, waits for them, and re-layouts, to_chunk(): v = jnp.swapaxes(v, 0, 1)  16.9 us
    transpose x3, local copies, waits for them, and re-layouts, to_expert(): v = jnp.swapaxes(v, 0, 1)  16.6 us
  transfers between devices with their start and end apart: 6, of which 6 were waited for; matrix products, arithmetic and copies ran while one was open for 3% of the time, Pallas kernels for 0%

profile of v1, /device:TPU:0, one launch (start us, length us, event | category | flops | bytes accessed | tf_op | source)
XLA Modules:
  0.0 803.5 jit_solution(7608984896195848699)
XLA Ops:
  18.1 11.7 %collective-permute-done = bf16[64,4224]{1,0:T(8,128)(2,1)S(1)} collective-permute-done((bf16[64,4224]{1,0:T(8,128)(2,1)S(1)}, bf16[64,4224]{1,0:T(8,128)(2,1)S(1)}, u32[]{:S(2)}, u32[]{:S(2)}) %collective-permute-start) | collective-permute-done | bytes 540704 | tf_op jit(solution)/shard_map/ppermute | solution.py:18
  31.6 24.5 %collective-permute-done.1 = bf16[128,4224]{1,0:T(8,128)(2,1)S(1)} collective-permute-done((bf16[128,4224]{1,0:T(8,128)(2,1)S(1)}, bf16[128,4224]{1,0:T(8,128)(2,1)S(1)}, u32[]{:S(2)}, u32[]{:S(2)}) %collective-permute-start.1) | collective-permute-done | bytes 1081376 | tf_op jit(solution)/shard_map/ppermute | solution.py:18
  57.4 95.9 %collective-permute-done.2 = bf16[256,4224]{1,0:T(8,128)(2,1)S(1)} collective-permute-done((bf16[256,4224]{1,0:T(8,128)(2,1)S(1)}, bf16[256,4224]{1,0:T(8,128)(2,1)S(1)}, u32[]{:S(2)}, u32[]{:S(2)}) %collective-permute-start.2) | collective-permute-done | bytes 2162720 | tf_op jit(solution)/shard_map/ppermute | solution.py:18
  161.2 42.5 %collective-permute-done.3 = bf16[512,4224]{1,0:T(8,128)(2,1)S(1)} collective-permute-done((bf16[512,4224]{1,0:T(8,128)(2,1)S(1)}, bf16[512,4224]{1,0:T(8,128)(2,1)S(1)}, u32[]{:S(2)}, u32[]{:S(2)}) %collective-permute-start.3) | collective-permute-done | bytes 4325408 | tf_op jit(solution)/shard_map/ppermute | solution.py:18
  211.0 187.4 %collective-permute-done.4 = bf16[1024,4224]{1,0:T(8,128)(2,1)} collective-permute-done((bf16[1024,4224]{1,0:T(8,128)(2,1)}, bf16[1024,4224]{1,0:T(8,128)(2,1)}, u32[]{:S(2)}, u32[]{:S(2)}) %collective-permute-start.4) | collective-permute-done | bytes 8650784 | tf_op jit(solution)/shard_map/ppermute | solution.py:18
  419.9 8.5 %constant_dynamic-slice_fusion = bf16[2048,4224]{1,0:T(8,128)(2,1)S(1)} fusion(bf16[4096,4224]{1,0:T(8,128)(2,1)} %constant_dynamic-update-slice_fusion.5, s32[]{:T(128)S(6)} %select_n.49), kind=kLoop, calls=%fused_computation.75 | loop fusion | bytes 34603012 | tf_op jit(solution)/shard_map/jit(_roll_dynamic)/dynamic_slice | solution.py:22
  435.8 9.0 %fusion.9 = bf16[8,256,2048]{2,1,0:T(8,128)(2,1)} fusion(bf16[8,256,256]{2,1,0:T(8,128)(2,1)S(1)} %convert_reduce_fusion, bf16[8,256,4224]{2,1,0:T(8,128)(2,1)} %bitcast.69), kind=kOutput, calls=%fused_computation.14 | convolution fusion | flops 2151677952 | bytes 17825792 | tf_op jit(solution)/shard_map/crt,ctd->crd/dot_general | solution.py:83
  444.9 9.0 %fusion.6 = bf16[8,256,2048]{2,1,0:T(8,128)(2,1)} fusion(bf16[8,256,256]{2,1,0:T(8,128)(2,1)S(1)} %convert_reduce_fusion, bf16[8,256,4224]{2,1,0:T(8,128)(2,1)} %bitcast.70), kind=kOutput, calls=%fused_computation.13 | convolution fusion | flops 2151677952 | bytes 17825792 | tf_op jit(solution)/shard_map/crt,ctd->crd/dot_general | solution.py:80
  453.9 8.3 %copy.102 = bf16[8,8,32,2048]{3,2,1,0:T(8,128)(2,1)} copy(bf16[8,8,32,2048]{3,2,0,1:T(8,128)(2,1)} %bitcast.74) | data formatting | bytes 16777216 | tf_op jit(solution)/shard_map/transpose | solution.py:71
  462.2 8.3 %copy.96 = bf16[8,8,32,2048]{3,2,1,0:T(8,128)(2,1)} copy(bf16[8,8,32,2048]{3,2,0,1:T(8,128)(2,1)} %bitcast.73) | data formatting | bytes 16777216 | tf_op jit(solution)/shard_map/transpose | solution.py:71
  470.5 8.2 %fusion.22 = f32[8,256,192]{1,2,0:T(8,128)S(1)} fusion(bf16[8,256,2048]{2,1,0:T(8,128)(2,1)} %bitcast.62, bf16[8,192,2048]{2,1,0:T(8,128)(2,1)} %param.12), kind=kOutput, calls=%fused_computation.77 | convolution fusion | flops 1610612736 | bytes 16252928 | tf_op jit(solution)/shard_map/erd,efd->erf/dot_general | solution.py:86
  478.7 18.9 %fusion.23 = f32[8,256,192]{1,2,0:T(8,128)} fusion(bf16[8,256,2048]{2,1,0:T(8,128)(2,1)S(1)} %bitcast.64, bf16[8,192,2048]{2,1,0:T(8,128)(2,1)} %param.13), kind=kOutput, calls=%fused_computation.78 | convolution fusion | flops 1610612736 | bytes 16252928 | tf_op jit(solution)/shard_map/erd,efd->erf/dot_general | solution.py:87
  497.7 10.0 %multiply_reduce_fusion = (f32[8,256]{1,0:T(8,128)S(1)}, f32[8,256,192]{1,2,0:T(8,128)}) fusion(f32[8,256,192]{1,2,0:T(8,128)} %fusion.23, f32[8,256,192]{1,2,0:T(8,128)S(1)} %fusion.22, bf16[8,256,2048]{2,1,0:T(8,128)(2,1)} %bitcast.77, bf16[8,192,2048]{2,1,0:T(8,128)(2,1)} %param.14), kind=kOutput, calls=%fused_computation.22 | convolution fusion | flops 1613363200 | bytes 19406848 | tf_op jit(solution)/shard_map/erd,efd->erf/dot_general | solution.py:88
  514.8 8.4 %convolution_convert_fusion = bf16[8,256,2048]{2,1,0:T(8,128)(2,1)} fusion(bf16[8,256,192]{1,2,0:T(8,128)(2,1)S(1)} %get-tuple-element.46, bf16[8,192,2048]{2,1,0:T(8,128)(2,1)} %param.14), kind=kOutput, calls=%fused_computation.12 | convolution fusion | flops 1614807040 | bytes 15466496 | tf_op jit(solution)/shard_map/erf,efd->erd/dot_general | solution.py:97
  523.2 8.4 %copy.99 = bf16[8,8,32,2048]{3,2,1,0:T(8,128)(2,1)} copy(bf16[8,8,32,2048]{3,2,0,1:T(8,128)(2,1)} %bitcast.72) | data formatting | bytes 16777216 | tf_op jit(solution)/shard_map/transpose | solution.py:76
  531.6 9.2 %convolution_convert_fusion.2 = bf16[8,256,2048]{2,1,0:T(8,128)(2,1)} fusion(bf16[8,256,256]{2,1,0:T(8,128)(2,1)S(1)} %convert_reduce_fusion, bf16[8,256,2048]{2,1,0:T(8,128)(2,1)} %bitcast.76), kind=kOutput, calls=%fused_computation.16 | convolution fusion | flops 2151677952 | bytes 17825792 | tf_op jit(solution)/shard_map/crt,crd->ctd/dot_general | solution.py:105
  540.8 8.2 %fusion.24 = f32[8,256,2048]{2,1,0:T(8,128)} fusion(bf16[8,256,192]{1,2,0:T(8,128)(2,1)S(1)} %get-tuple-element.47, bf16[8,192,2048]{2,1,0:T(8,128)(2,1)S(1)} %bitcast.81), kind=kOutput, calls=%fused_computation.79 | convolution fusion | flops 1610612736 | bytes 23855104 | tf_op jit(solution)/shard_map/erf,efd->erd/dot_general | solution.py:99
  548.9 13.5 %add_convert_fusion = bf16[8,256,2048]{2,1,0:T(8,128)(2,1)} fusion(f32[8,256,2048]{2,1,0:T(8,128)} %fusion.24, bf16[8,256,192]{1,2,0:T(8,128)(2,1)} %get-tuple-element.48, bf16[8,192,2048]{2,1,0:T(8,128)(2,1)} %param.13), kind=kOutput, calls=%fused_computation.3 | convolution fusion | flops 1619001344 | bytes 32243712 | tf_op jit(solution)/shard_map/erf,efd->erd/dot_general | solution.py:100
  562.4 8.4 %copy.103 = bf16[8,8,32,2048]{3,2,1,0:T(8,128)(2,1)} copy(bf16[8,8,32,2048]{3,2,0,1:T(8,128)(2,1)} %bitcast.79) | data formatting | bytes 16777216 | tf_op jit(solution)/shard_map/transpose | solution.py:76
  570.9 9.0 %convolution_convert_fusion.1 = bf16[8,256,2048]{2,1,0:T(8,128)(2,1)} fusion(bf16[8,256,256]{2,1,0:T(8,128)(2,1)S(1)} %convert_reduce_fusion, bf16[8,256,2048]{2,1,0:T(8,128)(2,1)} %bitcast.75), kind=kOutput, calls=%fused_computation.15 | convolution fusion | flops 2151677952 | bytes 17825792 | tf_op jit(solution)/shard_map/crt,crd->ctd/dot_general | solution.py:106
  580.2 13.8 %fusion.1 = bf16[8,256,4224]{2,1,0:T(8,128)(2,1)} fusion(bf16[8,256,4]{2,1,0:T(8,128)(2,1)S(1)} %copy.123, bf16[8,256,2048]{2,1,0:T(8,128)(2,1)} %convolution_convert_fusion.1, bf16[8,256,2048]{2,1,0:T(8,128)(2,1)} %convolution_convert_fusion.2), kind=kLoop, calls=%fused_computation.2 | loop fusion | flops 69206016 | bytes 34095104 | tf_op jit(solution)/shard_map/concatenate | solution.py:110
  594.1 8.1 %convolution_convert_fusion.3 = bf16[8,192,2048]{2,1,0:T(8,128)(2,1)} fusion(bf16[8,256,192]{1,2,0:T(8,128)(2,1)S(1)} %get-tuple-element.46, bf16[8,256,2048]{2,1,0:T(8,128)(2,1)} %bitcast.78), kind=kOutput, calls=%fused_computation.17 | convolution fusion | flops 1613758464 | bytes 15466496 | tf_op jit(solution)/shard_map/erf,erd->efd/dot_general | solution.py:104
  602.2 8.8 %convolution_convert_fusion.4 = bf16[8,192,2048]{2,1,0:T(8,128)(2,1)} fusion(bf16[8,256,192]{1,2,0:T(8,128)(2,1)S(1)} %copy-done.6, bf16[8,256,2048]{2,1,0:T(8,128)(2,1)} %bitcast.63), kind=kOutput, calls=%fused_computation.18 | convolution fusion | flops 1613758464 | bytes 15466496 | tf_op jit(solution)/shard_map/erf,erd->efd/dot_general | solution.py:103
  615.5 177.7 %reduce-scatter.4.cloned.1.call-done = bf16[64,4224]{1,0:T(8,128)(2,1)} async-done(((bf16[2048,4224]{1,0:T(8,128)(2,1)}), bf16[64,4224]{1,0:T(8,128)(2,1)}) %reduce-scatter.4.cloned.1.call-update) | async-done | bytes 540688
  (87 shorter events, 73.4 us)
Async XLA Ops:
  7.2 146.1 %copy-start.7 = (bf16[64,2048]{1,0:T(8,128)(2,1)S(1)}, bf16[64,2048]{1,0:T(8,128)(2,1)}, u32[]{:S(2)}) copy-start(bf16[64,2048]{1,0:T(8,128)(2,1)} %param.15) | copy-start | bytes 786436
  7.2 786.0 %reduce-scatter.4.cloned.1.call-start = ((), (), s32[]{:S(2)}) async-start(), calls=%async_computation.1 | async-start | bytes 17842176
  9.5 143.8 %copy-start.8 = (bf16[64,2048]{1,0:T(8,128)(2,1)S(1)}, bf16[64,2048]{1,0:T(8,128)(2,1)}, u32[]{:S(2)}) copy-start(bf16[64,2048]{1,0:T(8,128)(2,1)} %param.8) | copy-start | bytes 786436
  11.7 18.1 %collective-permute-start = (bf16[64,4224]{1,0:T(8,128)(2,1)S(1)}, bf16[64,4224]{1,0:T(8,128)(2,1)S(1)}, u32[]{:S(2)}, u32[]{:S(2)}) collective-permute-start(bf16[64,4224]{1,0:T(8,128)(2,1)S(1)} %get-tuple-element.59), channel_id=1, source_target_pairs={{0,31},{1,0},{2,1},{3,2},{4,3},{5,4},{6,5},{7,6},{8,7},{9,8},{10,9... | collective-permute-start | bytes 1622024 | tf_op jit(solution)/shard_map/ppermute | solution.py:18
  29.8 129.1 %copy-start.4 = (bf16[64,4224]{1,0:T(8,128)(2,1)}, bf16[64,4224]{1,0:T(8,128)(2,1)S(1)}, u32[]{:S(2)}) copy-start(bf16[64,4224]{1,0:T(8,128)(2,1)S(1)} %collective-permute-done) | copy-start | bytes 1622020
  31.1 25.0 %collective-permute-start.1 = (bf16[128,4224]{1,0:T(8,128)(2,1)S(1)}, bf16[128,4224]{1,0:T(8,128)(2,1)S(1)}, u32[]{:S(2)}, u32[]{:S(2)}) collective-permute-start(bf16[128,4224]{1,0:T(8,128)(2,1)S(1)} %pad_maximum_fusion.2), channel_id=1, source_target_pairs={{0,30},{1,31},{2,0},{3,1},{4,2},{5,3},{6,4},{7,5},{8,6},{9,7},{10,... | collective-permute-start | bytes 3244040 | tf_op jit(solution)/shard_map/ppermute | solution.py:18
  57.3 96.0 %collective-permute-start.2 = (bf16[256,4224]{1,0:T(8,128)(2,1)S(1)}, bf16[256,4224]{1,0:T(8,128)(2,1)S(1)}, u32[]{:S(2)}, u32[]{:S(2)}) collective-permute-start(bf16[256,4224]{1,0:T(8,128)(2,1)S(1)} %pad_maximum_fusion.1), channel_id=1, source_target_pairs={{0,28},{1,29},{2,30},{3,31},{4,0},{5,1},{6,2},{7,3},{8,4},{9,5},{1... | collective-permute-start | bytes 6488072 | tf_op jit(solution)/shard_map/ppermute | solution.py:18
  155.5 48.2 %collective-permute-start.3 = (bf16[512,4224]{1,0:T(8,128)(2,1)S(1)}, bf16[512,4224]{1,0:T(8,128)(2,1)S(1)}, u32[]{:S(2)}, u32[]{:S(2)}) collective-permute-start(bf16[512,4224]{1,0:T(8,128)(2,1)S(1)} %pad_maximum_fusion), channel_id=1, source_target_pairs={{0,24},{1,25},{2,26},{3,27},{4,28},{5,29},{6,30},{7,31},{8,0},{9,1... | collective-permute-start | bytes 12976136 | tf_op jit(solution)/shard_map/ppermute | solution.py:18
  203.7 2.1 copy-start.2
  209.7 188.7 %collective-permute-start.4 = (bf16[1024,4224]{1,0:T(8,128)(2,1)}, bf16[1024,4224]{1,0:T(8,128)(2,1)}, u32[]{:S(2)}, u32[]{:S(2)}) collective-permute-start(bf16[1024,4224]{1,0:T(8,128)(2,1)} %get-tuple-element.44), channel_id=1, source_target_pairs={{0,16},{1,17},{2,18},{3,19},{4,20},{5,21},{6,22},{7,23},{8,24},{9,... | collective-permute-start | bytes 25952264 | tf_op jit(solution)/shard_map/ppermute | solution.py:18
  398.4 7.5 copy-start.9
  398.4 8.3 %copy-start.5 = (bf16[64,4224]{1,0:T(8,128)(2,1)S(1)}, bf16[64,4224]{1,0:T(8,128)(2,1)}, u32[]{:S(2)}) copy-start(bf16[64,4224]{1,0:T(8,128)(2,1)} %copy-done.4) | copy-start | bytes 1622020
  405.8 4.3 copy-start.3
  428.3 5.9 copy-start.1
  470.5 8.2 %copy-start = (bf16[8,8,32,2048]{3,2,1,0:T(8,128)(2,1)S(1)}, bf16[8,8,32,2048]{3,2,1,0:T(8,128)(2,1)}, u32[]{:S(2)}) copy-start(bf16[8,8,32,2048]{3,2,1,0:T(8,128)(2,1)} %copy.96) | copy-start | bytes 25165828
  478.7 18.9 %copy-start.10 = (f32[8,256,192]{1,2,0:T(8,128)}, f32[8,256,192]{1,2,0:T(8,128)S(1)}, u32[]{:S(2)}) copy-start(f32[8,256,192]{1,2,0:T(8,128)S(1)} %fusion.22) | copy-start | bytes 4718596
  523.2 17.6 %slice-start.2 = ((s8[6291456]{0:T(1024)(128)(4,1)}), s8[2097152]{0:T(1024)(128)(4,1)S(1)}, s32[]{:S(2)}) async-start(s8[6291456]{0:T(1024)(128)(4,1)} %bitcast.80), calls=%async_computation.4 | async-start | bytes 4194304
  531.6 9.2 %slice-start.3 = ((s8[6291456]{0:T(1024)(128)(4,1)}), s8[4194304]{0:T(1024)(128)(4,1)S(1)}, s32[]{:S(2)}) async-start(s8[6291456]{0:T(1024)(128)(4,1)} %bitcast.80), calls=%async_computation.5 | async-start | bytes 8388608
  594.1 8.1 %copy-start.6 = (bf16[8,256,192]{1,2,0:T(8,128)(2,1)S(1)}, bf16[8,256,192]{1,2,0:T(8,128)(2,1)}, u32[]{:S(2)}) copy-start(bf16[8,256,192]{1,2,0:T(8,128)(2,1)} %get-tuple-element.48) | copy-start | bytes 2359300
  594.1 16.8 %slice-start = ((s8[8388608]{0:T(1024)(128)(4,1)}), s8[4194304]{0:T(1024)(128)(4,1)S(1)}, s32[]{:S(2)}) async-start(s8[8388608]{0:T(1024)(128)(4,1)} %bitcast.65), calls=%async_computation.2 | async-start | bytes 8388608
  602.2 8.8 %slice-start.1 = ((s8[8388608]{0:T(1024)(128)(4,1)}), s8[4194304]{0:T(1024)(128)(4,1)S(1)}, s32[]{:S(2)}) async-start(s8[8388608]{0:T(1024)(128)(4,1)} %bitcast.65), calls=%async_computation.3 | async-start | bytes 8388608
Sparse Core Ops, SparseCore 0:
  594.2 198.9 reduce-scatter.3
